TPU v7x, 32 devices: a whole 2x2x4 slice. The times are simulated.
32 devices in a mesh: dp: 8 (over z, x), tensor: 4 (over y, core).
Axes of the slice: x: 2, y: 2, z: 4, core: 2. Of those that a mesh axis runs over, the one named last changes fastest.
Arguments:
- inputs: bfloat16 [8192, 4096], P('dp'), may hold values from -6 to 6
- out_grads: bfloat16 [8192, 6144], P('dp', 'tensor'), may hold values from -0.01953125 to 0.01953125
- left_factor: float32 [4096, 4096], P('dp', 'tensor'), may hold values from -6 to 6
- right_factor: float32 [6144, 6144], P('dp', 'tensor'), may hold values from -6 to 6
- left_basis: float32 [4096, 4096], P('dp', 'tensor'), may hold values from -0.09375 to 0.09375
- right_basis: float32 [6144, 6144], P('dp', 'tensor'), may hold values from -0.078125 to 0.078125
Outputs:
- left_new: float32 [4096, 4096], P('dp', 'tensor')
- right_new: float32 [6144, 6144], P('dp', 'tensor')
- rotated: float32 [4096, 6144], P('dp', 'tensor')
All inputs are finite; a program needn't handle non-finite values.
Results may differ from a plain program's by a relative error of at most 0.019.
Values may be sent and summed in bfloat16 or wider, within the bound.
A program may use at most 192 MiB of HBM per device.

v0:
```python
import jax
import jax.numpy as jnp
from jax import lax
from jax.sharding import PartitionSpec as P

F32 = jnp.float32
BF16 = jnp.bfloat16


def mm(a, b, ca, cb):
    return lax.dot_general(a, b, (((ca,), (cb,)), ((), ())), preferred_element_type=F32)


def spread(block, owner, n_dp, n_t, later):
    me = lax.axis_index("tensor")
    mine = me ^ owner(lax.axis_index("dp"))
    step = n_t // 2
    while step:
        pairs = []
        for d in range(n_dp):
            for k in range(0, n_t, 2 * step):
                src = owner(d) ^ k
                pairs.append((d * n_t + src, d * n_t + (src ^ step)))
        got = lax.ppermute(block, ("dp", "tensor"), pairs)
        if step == n_t // 2:
            got, later = lax.optimization_barrier((got, later))
        block = jnp.where(mine % (2 * step) == step, got, block)
        step //= 2
    return (block, later)


def gather_by_permutes(block, axis, n, hop):
    count = n // hop
    me = lax.axis_index(axis)
    group = me // hop
    got = [block]
    for r in range(1, count):
        pairs = [(p, (p // hop + r) % count * hop + p % hop) for p in range(n)]
        got.append(lax.ppermute(block, axis, pairs))
    return (got, group, count)


def in_order(got, group, count):
    out = jnp.zeros((count,) + got[0].shape, got[0].dtype)
    for r in range(count):
        out = lax.dynamic_update_slice_in_dim(
            out, got[r][None], lax.rem(group - r + count, count), 0
        )
    return out


def shards(inputs, out_grads, left_factor, right_factor, left_basis, right_basis):
    n_dp, n_t = (lax.axis_size("dp"), lax.axis_size("tensor"))
    krows, kcols = left_factor.shape
    mrows, mcols = right_factor.shape
    dp = lax.axis_index("dp")
    right_low = right_basis.astype(BF16)
    left_low = left_basis.astype(BF16)
    zgot, zgroup, zcount = gather_by_permutes(right_low, "dp", n_dp, 2)
    lgot, lgroup, lcount = gather_by_permutes(left_low, "tensor", n_t, 1)
    partial = mm(inputs, out_grads, 0, 0).astype(BF16)
    summed = lax.psum_scatter(partial, "dp", scatter_dimension=0, tiled=True)
    left_rows = in_order(lgot, lgroup, lcount)
    left_cols = lax.all_to_all(
        left_rows.reshape(n_t, krows, kcols // krows, krows)
        .transpose(0, 2, 1, 3)
        .reshape(n_dp, krows, krows),
        "dp",
        split_axis=0,
        concat_axis=0,
        tiled=True,
    ).reshape(n_dp * krows, krows)
    cross = [(p, p ^ 1) for p in range(n_dp)]
    early = len(zgot) // 2
    first = [lax.ppermute(z, "dp", cross) for z in zgot[:early]]
    summed, zgot, first, left_cols = lax.optimization_barrier((summed, zgot, first, left_cols))
    col_panel = lax.all_gather(summed, "dp", axis=0, tiled=True)
    last = [lax.ppermute(z, "dp", cross) for z in zgot[early:]]
    basis_panel = jnp.zeros((n_dp,) + right_low.shape, BF16)
    for r in range(early):
        at = lax.rem(zgroup - r + zcount, zcount) * 2 + lax.rem(dp, 2)
        basis_panel = lax.dynamic_update_slice_in_dim(basis_panel, zgot[r][None], at, 0)
        basis_panel = lax.dynamic_update_slice_in_dim(basis_panel, first[r][None], at ^ 1, 0)
    col_panel, last, basis_panel = lax.optimization_barrier((col_panel, last, basis_panel))
    for r in range(early, zcount):
        at = lax.rem(zgroup - r + zcount, zcount) * 2 + lax.rem(dp, 2)
        basis_panel = lax.dynamic_update_slice_in_dim(basis_panel, zgot[r][None], at, 0)
        basis_panel = lax.dynamic_update_slice_in_dim(basis_panel, last[r - early][None], at ^ 1, 0)
    basis_panel = basis_panel.reshape(n_dp * mrows, mcols)
    turned = mm(left_cols, col_panel, 0, 0).astype(BF16)
    turned, summed = lax.optimization_barrier((turned, summed))
    turned_rows = lax.all_gather(turned, "tensor", axis=1, tiled=True)
    own = lax.dynamic_slice_in_dim(col_panel, lax.rem(dp * mrows, mcols), mrows, 1)
    parts = jnp.einsum(
        "jkc,rc->jrk", col_panel.reshape(n_t, kcols, mcols), summed, preferred_element_type=F32
    ).astype(BF16)
    own, parts = spread(own, lambda d: d * mrows // mcols, n_dp, n_t, parts)
    gram_left = lax.psum_scatter(
        parts.reshape(n_t * krows, kcols), "tensor", scatter_dimension=0, tiled=True
    ).astype(F32)
    left_new = 0.95 * left_factor + 0.05 * gram_left
    right_new = 0.95 * right_factor + 0.05 * mm(own, col_panel, 0, 0)
    rotated = mm(turned_rows, basis_panel, 1, 0)
    return (left_new, right_new, rotated)


def solution(mesh):
    spec = P("dp", "tensor")
    return jax.shard_map(
        shards,
        mesh=mesh,
        in_specs=(P("dp", None), spec, spec, spec, spec, spec),
        out_specs=(spec, spec, spec),
        check_vma=False,
    )
```

profile of v0, /device:TPU:25, one launch (start us, length us, event | category | flops | bytes accessed | tf_op | source)
XLA Modules:
  0.0 908.6 jit_solution(4041019502134151689)
XLA Ops:
  7.2 1.8 copy-done
  9.1 19.2 %convolution_convert_fusion = bf16[4096,1536]{1,0:T(8,128)(2,1)} fusion(bf16[1024,4096]{1,0:T(8,128)(2,1)} %param.6, bf16[1024,1536]{1,0:T(8,128)(2,1)S(1)} %copy-done), kind=kOutput, calls=%fused_computation | convolution fusion | flops 12891193344 | bytes 24117248 | tf_op jit(solution)/shard_map/dot_general | solution.py:11
  28.3 2.5 broadcast_in_dim.42
  30.8 1.3 bitcast_dynamic-update-slice_fusion.11
  32.1 1.8 collective-permute-start.5
  33.9 0.2 collective-permute-start.6
  34.3 22.0 %collective-permute-done.5 = bf16[512,1024]{1,0:T(8,128)(2,1)} collective-permute-done((bf16[512,1024]{1,0:T(8,128)(2,1)S(1)}, bf16[512,1024]{1,0:T(8,128)(2,1)}, u32[]{:S(2)}, u32[]{:S(2)}) %collective-permute-start.5) | collective-permute-done | bytes 1048608 | tf_op jit(solution)/shard_map/ppermute | solution.py:39
  56.3 2.3 bitcast_dynamic-update-slice_fusion.10
  58.6 21.3 %collective-permute-done.6 = bf16[512,1024]{1,0:T(8,128)(2,1)S(1)} collective-permute-done((bf16[512,1024]{1,0:T(8,128)(2,1)S(1)}, bf16[512,1024]{1,0:T(8,128)(2,1)S(1)}, u32[]{:S(2)}, u32[]{:S(2)}) %collective-permute-start.6) | collective-permute-done | bytes 1048608 | tf_op jit(solution)/shard_map/ppermute | solution.py:39
  79.8 1.0 bitcast_dynamic-update-slice_fusion.9
  80.9 1.0 bitcast_dynamic-update-slice_fusion.8
  81.9 2.5 fusion.6
  84.5 2.3 pad_maximum_fusion
  86.8 5.6 all-to-all-start
  92.3 2.6 convert_element_type.22
  95.1 1.3 collective-permute-start.1
  96.5 0.3 collective-permute-start.2
  96.7 1.2 collective-permute-start.3
  97.9 159.0 %collective-permute-done = bf16[768,1536]{1,0:T(8,128)(2,1)S(1)} collective-permute-done((bf16[768,1536]{1,0:T(8,128)(2,1)S(1)}, bf16[768,1536]{1,0:T(8,128)(2,1)S(1)}, u32[]{:S(2)}, u32[]{:S(2)}) %collective-permute-start) | collective-permute-done | bytes 2359328 | tf_op jit(solution)/shard_map/ppermute | solution.py:39
  256.9 1.1 collective-permute-start.4
  258.0 224.0 %collective-permute-done.1 = bf16[768,1536]{1,0:T(8,128)(2,1)S(1)} collective-permute-done((bf16[768,1536]{1,0:T(8,128)(2,1)S(1)}, bf16[768,1536]{1,0:T(8,128)(2,1)S(1)}, u32[]{:S(2)}, u32[]{:S(2)}) %collective-permute-start.1) | collective-permute-done | bytes 2359328 | tf_op jit(solution)/shard_map/ppermute | solution.py:39
  482.1 1.4 copy-done.4
  483.5 0.7 copy-done.2
  484.2 1.4 copy-done.7
  485.7 1.5 collective-permute-start.8
  487.3 6.8 broadcast_in_dim.47
  494.1 1.5 bitcast_dynamic-update-slice_fusion.7
  495.6 1.3 copy-done.8
  496.9 1.6 bitcast_dynamic-update-slice_fusion.6
  498.5 1.5 bitcast_dynamic-update-slice_fusion.5
  500.0 3.3 bitcast_dynamic-update-slice_fusion.4
  503.3 52.1 %collective-permute-done.8 = bf16[768,1536]{1,0:T(8,128)(2,1)} collective-permute-done((bf16[768,1536]{1,0:T(8,128)(2,1)}, bf16[768,1536]{1,0:T(8,128)(2,1)}, u32[]{:S(2)}, u32[]{:S(2)}) %collective-permute-start.8) | collective-permute-done | bytes 2359328 | tf_op jit(solution)/shard_map/ppermute | solution.py:78
  555.4 93.4 %collective-permute-done.9 = bf16[768,1536]{1,0:T(8,128)(2,1)} collective-permute-done((bf16[768,1536]{1,0:T(8,128)(2,1)}, bf16[768,1536]{1,0:T(8,128)(2,1)}, u32[]{:S(2)}, u32[]{:S(2)}) %collective-permute-start.9) | collective-permute-done | bytes 2359328 | tf_op jit(solution)/shard_map/ppermute | solution.py:78
  648.8 60.1 %all-gather.3.cloned.1.call-done = bf16[4096,1536]{1,0:T(8,128)(2,1)} async-done(((bf16[512,1536]{1,0:T(8,128)(2,1)}), bf16[4096,1536]{1,0:T(8,128)(2,1)}) %all-gather.3.cloned.1.call-update) | async-done | bytes 12582928 | tf_op jit(solution)/shard_map/all_gather | solution.py:77
  708.9 11.8 %convolution_convert_fusion.1 = bf16[512,1536]{1,0:T(8,128)(2,1)} fusion(bf16[4096,512]{1,0:T(8,128)(2,1)} %bitcast.5, bf16[4096,1536]{1,0:T(8,128)(2,1)} %all-gather.3.cloned.1.call-done), kind=kOutput, calls=%fused_computation.8 | convolution fusion | flops 6443237376 | bytes 18350080 | tf_op jit(solution)/shard_map/dot_general | solution.py:11
  721.0 9.7 %constant_dynamic-slice_fusion = bf16[4096,768]{1,0:T(8,128)(2,1)} fusion(bf16[4096,1536]{1,0:T(8,128)(2,1)} %all-gather.3.cloned.1.call-done, s32[]{:T(128)S(6)} %select_n.81), kind=kLoop, calls=%fused_computation.23 | loop fusion | bytes 12582916 | tf_op jit(solution)/shard_map/dynamic_slice | solution.py:93
  730.7 1.3 collective-permute-start.10
  732.0 19.4 %convert_bitcast_fusion = bf16[4,512,1024]{2,1,0:T(8,128)(2,1)} fusion(bf16[4,1024,1536]{2,1,0:T(8,128)(2,1)} %bitcast.43, bf16[512,1536]{1,0:T(8,128)(2,1)S(1)} %copy-done.10), kind=kOutput, calls=%fused_computation.7 | convolution fusion | flops 6444548096 | bytes 18350080 | tf_op jit(solution)/shard_map/jkc,rc->jrk/dot_general | solution.py:94
  751.4 83.8 %collective-permute-done.10 = bf16[4096,768]{1,0:T(8,128)(2,1)} collective-permute-done((bf16[4096,768]{1,0:T(8,128)(2,1)}, bf16[4096,768]{1,0:T(8,128)(2,1)}, u32[]{:S(2)}, u32[]{:S(2)}) %collective-permute-start.10) | collective-permute-done | bytes 6291488 | tf_op jit(solution)/shard_map/ppermute | solution.py:24
  835.3 12.0 %broadcast_select_fusion = bf16[4096,768]{1,0:T(8,128)(2,1)} fusion(bf16[4096,768]{1,0:T(8,128)(2,1)} %collective-permute-done.10, pred[]{:T(512)S(6)} %eq.10, bf16[4096,1536]{1,0:T(8,128)(2,1)} %all-gather.3.cloned.1.call-done, s32[]{:T(128)S(6)} %select_n.81), kind=kLoop, calls=%fused_computation.3 | loop fusion | flops 3145728 | bytes 18874372 | tf_op jit(solution)/shard_map/jit(_where)/select_n | solution.py:27
  847.2 3.9 collective-permute-start.11
  851.1 3.4 bitcast_dynamic-update-slice_fusion.3
  854.6 3.3 bitcast_dynamic-update-slice_fusion.2
  857.9 1.6 bitcast_dynamic-update-slice_fusion.1
  859.4 3.7 bitcast_dynamic-update-slice_fusion
  863.1 16.9 %fusion.7 = f32[512,1536]{1,0:T(8,128)} fusion(bf16[512,6144]{1,0:T(8,128)(2,1)} %all-gather.5.cloned.1.call-done, bf16[6144,1536]{1,0:T(8,128)(2,1)} %bitcast.18), kind=kOutput, calls=%fused_computation.25 | convolution fusion | flops 9663676416 | bytes 28311552 | tf_op jit(solution)/shard_map/dot_general | solution.py:11
  880.0 18.3 %multiply_add_fusion = f32[768,1536]{1,0:T(8,128)} fusion(f32[768,1536]{1,0:T(8,128)} %param.9, bf16[4096,1536]{1,0:T(8,128)(2,1)} %all-gather.3.cloned.1.call-done, bf16[4096,768]{1,0:T(8,128)(2,1)} %collective-permute-done.11, bf16[4096,768]{1,0:T(8,128)(2,1)} %broadcast_select_fusion, pred[]{:T(512)S(6)} %eq.9), kind=kOutput, calls=%fused_computation.5 | convolution fusion | flops 9670361088 | bytes 34603008 | tf_op jit(solution)/shard_map/dot_general | solution.py:11
  898.3 3.7 multiply_add_fusion.1
  (37 shorter events, 0.9 us)
Async XLA Ops:
  7.2 1.9 copy-start
  7.2 478.4 %reduce-scatter.3.cloned.1.call-start = ((), (), s32[]{:S(2)}) async-start(), calls=%async_computation.3 | async-start | bytes 14155776 | tf_op jit(solution)/shard_map/reduce_scatter | solution.py:62
  28.2 2.6 copy-start.9
  32.1 24.2 %collective-permute-start.5 = (bf16[512,1024]{1,0:T(8,128)(2,1)S(1)}, bf16[512,1024]{1,0:T(8,128)(2,1)}, u32[]{:S(2)}, u32[]{:S(2)}) collective-permute-start(bf16[512,1024]{1,0:T(8,128)(2,1)S(1)} %get-tuple-element.36), channel_id=1, source_target_pairs={{0,1},{1,2},{2,3},{3,0},{4,5},{5,6},{6,7},{7,4},{8,9},{9,10},{10,1... | collective-permute-start | bytes 3145736 | tf_op jit(solution)/shard_map/ppermute | solution.py:39
  33.9 46.0 %collective-permute-start.6 = (bf16[512,1024]{1,0:T(8,128)(2,1)S(1)}, bf16[512,1024]{1,0:T(8,128)(2,1)S(1)}, u32[]{:S(2)}, u32[]{:S(2)}) collective-permute-start(bf16[512,1024]{1,0:T(8,128)(2,1)S(1)} %get-tuple-element.36), channel_id=1, source_target_pairs={{0,2},{1,3},{2,0},{3,1},{4,6},{5,7},{6,4},{7,5},{8,10},{9,11},{10,... | collective-permute-start | bytes 3145736 | tf_op jit(solution)/shard_map/ppermute | solution.py:39
  34.1 46.8 %collective-permute-start.7 = (bf16[512,1024]{1,0:T(8,128)(2,1)S(1)}, bf16[512,1024]{1,0:T(8,128)(2,1)S(1)}, u32[]{:S(2)}, u32[]{:S(2)}) collective-permute-start(bf16[512,1024]{1,0:T(8,128)(2,1)S(1)} %get-tuple-element.36), channel_id=1, source_target_pairs={{0,3},{1,0},{2,1},{3,2},{4,7},{5,4},{6,5},{7,6},{8,11},{9,8},{10,9... | collective-permute-start | bytes 3145736 | tf_op jit(solution)/shard_map/ppermute | solution.py:39
  86.8 398.8 %all-to-all-start = ((bf16[8,512,512]{2,1,0:T(8,128)(2,1)}), bf16[8,512,512]{2,1,0:T(8,128)(2,1)}, u32[]{:S(2)}, u32[]{:S(2)}) async-start(bf16[8,512,512]{2,1,0:T(8,128)(2,1)} %bitcast.42), calls=%async_computation.1 | async-start | bytes 8388608 | tf_op jit(solution)/shard_map/all_to_all | solution.py:64
  92.3 616.6 %all-gather.3.cloned.1.call-start = ((), (), s32[]{:S(2)}) async-start(), calls=%async_computation.4 | async-start | bytes 14155776 | tf_op jit(solution)/shard_map/all_gather | solution.py:77
  94.9 161.9 %collective-permute-start = (bf16[768,1536]{1,0:T(8,128)(2,1)S(1)}, bf16[768,1536]{1,0:T(8,128)(2,1)S(1)}, u32[]{:S(2)}, u32[]{:S(2)}) collective-permute-start(bf16[768,1536]{1,0:T(8,128)(2,1)S(1)} %convert_element_type.22), channel_id=1, source_target_pairs={{0,8},{4,12},{8,16},{12,20},{16,24},{20,28},{24,0},{28,4},{1,9},{5... | collective-permute-start | bytes 7077896 | tf_op jit(solution)/shard_map/ppermute | solution.py:39
  95.1 386.9 %collective-permute-start.1 = (bf16[768,1536]{1,0:T(8,128)(2,1)S(1)}, bf16[768,1536]{1,0:T(8,128)(2,1)S(1)}, u32[]{:S(2)}, u32[]{:S(2)}) collective-permute-start(bf16[768,1536]{1,0:T(8,128)(2,1)S(1)} %convert_element_type.22), channel_id=1, source_target_pairs={{0,16},{4,20},{8,24},{12,28},{16,0},{20,4},{24,8},{28,12},{1,17},{... | collective-permute-start | bytes 7077896 | tf_op jit(solution)/shard_map/ppermute | solution.py:39
  96.5 385.6 %collective-permute-start.2 = (bf16[768,1536]{1,0:T(8,128)(2,1)S(1)}, bf16[768,1536]{1,0:T(8,128)(2,1)S(1)}, u32[]{:S(2)}, u32[]{:S(2)}) collective-permute-start(bf16[768,1536]{1,0:T(8,128)(2,1)S(1)} %convert_element_type.22), channel_id=1, source_target_pairs={{0,24},{4,28},{8,0},{12,4},{16,8},{20,12},{24,16},{28,20},{1,25},{... | collective-permute-start | bytes 7077896 | tf_op jit(solution)/shard_map/ppermute | solution.py:39
  96.7 385.3 %collective-permute-start.3 = (bf16[768,1536]{1,0:T(8,128)(2,1)S(1)}, bf16[768,1536]{1,0:T(8,128)(2,1)S(1)}, u32[]{:S(2)}, u32[]{:S(2)}) collective-permute-start(bf16[768,1536]{1,0:T(8,128)(2,1)S(1)} %convert_element_type.22), channel_id=1, source_target_pairs={{0,4},{4,0},{8,12},{12,8},{16,20},{20,16},{24,28},{28,24},{1,5},{5... | collective-permute-start | bytes 7077896 | tf_op jit(solution)/shard_map/ppermute | solution.py:75
  256.9 225.2 %copy-start.5 = (bf16[768,1536]{1,0:T(8,128)(2,1)}, bf16[768,1536]{1,0:T(8,128)(2,1)S(1)}, u32[]{:S(2)}) copy-start(bf16[768,1536]{1,0:T(8,128)(2,1)S(1)} %collective-permute-done) | copy-start | bytes 7077892
  256.9 228.7 %collective-permute-start.4 = (bf16[768,1536]{1,0:T(8,128)(2,1)S(1)}, bf16[768,1536]{1,0:T(8,128)(2,1)}, u32[]{:S(2)}, u32[]{:S(2)}) collective-permute-start(bf16[768,1536]{1,0:T(8,128)(2,1)S(1)} %collective-permute-done), channel_id=1, source_target_pairs={{0,4},{4,0},{8,12},{12,8},{16,20},{20,16},{24,28},{28,24},{1,5},{5... | collective-permute-start | bytes 7077896 | tf_op jit(solution)/shard_map/ppermute | solution.py:75
  482.0 1.4 copy-start.4
  482.1 2.1 copy-start.2
  484.2 1.4 copy-start.7
  485.6 377.5 %all-gather.5.cloned.1.call-start = ((), (), s32[]{:S(2)}) async-start(), calls=%async_computation.6 | async-start | bytes 7864320 | tf_op jit(solution)/shard_map/all_gather | solution.py:92
  485.7 69.7 %collective-permute-start.8 = (bf16[768,1536]{1,0:T(8,128)(2,1)}, bf16[768,1536]{1,0:T(8,128)(2,1)}, u32[]{:S(2)}, u32[]{:S(2)}) collective-permute-start(bf16[768,1536]{1,0:T(8,128)(2,1)} %copy-done.4), channel_id=1, source_target_pairs={{0,4},{4,0},{8,12},{12,8},{16,20},{20,16},{24,28},{28,24},{1,5},{5... | collective-permute-start | bytes 7077896 | tf_op jit(solution)/shard_map/ppermute | solution.py:78
  487.2 161.6 %collective-permute-start.9 = (bf16[768,1536]{1,0:T(8,128)(2,1)}, bf16[768,1536]{1,0:T(8,128)(2,1)}, u32[]{:S(2)}, u32[]{:S(2)}) collective-permute-start(bf16[768,1536]{1,0:T(8,128)(2,1)} %copy-done.2), channel_id=1, source_target_pairs={{0,4},{4,0},{8,12},{12,8},{16,20},{20,16},{24,28},{28,24},{1,5},{5... | collective-permute-start | bytes 7077896 | tf_op jit(solution)/shard_map/ppermute | solution.py:78
  494.1 2.8 copy-start.8
  494.1 4.4 copy-start.6
  720.7 177.6 %reduce-scatter.5.cloned.1.call-start = ((), (), s32[]{:S(2)}) async-start(), calls=%async_computation.5 | async-start | bytes 5242880 | tf_op jit(solution)/shard_map/reduce_scatter | solution.py:98
  721.0 11.0 %copy-start.10 = (bf16[512,1536]{1,0:T(8,128)(2,1)S(1)}, bf16[512,1536]{1,0:T(8,128)(2,1)}, u32[]{:S(2)}) copy-start(bf16[512,1536]{1,0:T(8,128)(2,1)} %reduce-scatter.3.cloned.1.call-done) | copy-start | bytes 4718596
  730.7 104.5 %collective-permute-start.10 = (bf16[4096,768]{1,0:T(8,128)(2,1)}, bf16[4096,768]{1,0:T(8,128)(2,1)}, u32[]{:S(2)}, u32[]{:S(2)}) collective-permute-start(bf16[4096,768]{1,0:T(8,128)(2,1)} %constant_dynamic-slice_fusion), channel_id=1, source_target_pairs={{0,2},{4,6},{9,11},{13,15},{18,16},{22,20},{27,25},{31,29}} | collective-permute-start | bytes 18874376 | tf_op jit(solution)/shard_map/ppermute | solution.py:24
  847.2 32.8 %collective-permute-start.11 = (bf16[4096,768]{1,0:T(8,128)(2,1)}, bf16[4096,768]{1,0:T(8,128)(2,1)}, u32[]{:S(2)}, u32[]{:S(2)}) collective-permute-start(bf16[4096,768]{1,0:T(8,128)(2,1)} %broadcast_select_fusion), channel_id=1, source_target_pairs={{0,1},{2,3},{4,5},{6,7},{9,8},{11,10},{13,12},{15,14},{18,19},{16,... | collective-permute-start | bytes 18874376 | tf_op jit(solution)/shard_map/ppermute | solution.py:24
  851.1 6.7 copy-start.3
  880.0 22.1 %copy-start.1 = (bf16[1024,1536]{1,0:T(8,128)(2,1)S(1)}, bf16[1024,1536]{1,0:T(8,128)(2,1)}, u32[]{:S(2)}) copy-start(bf16[1024,1536]{1,0:T(8,128)(2,1)} %param.7) | copy-start | bytes 9437188
Sparse Core Ops, SparseCore 0:
  28.4 407.5 reduce-scatter.2
  485.7 223.0 all-gather.2
  720.9 65.4 all-gather.4
  851.3 44.1 reduce-scatter.4
where the time goes:
time: 909 us
  waiting for transfers between devices  716 us (79%)
  matrix products  85.6 us (9%)
  local copies, waits for them, and re-layouts  52.5 us (6%)
  other arithmetic  21.9 us (2%)
  starting transfers between devices  18.9 us (2%)
  between operations  14 us (2%)
    ppermute x6, waiting for transfers between devices, gather_by_permutes(): got.append(lax.ppermute(block, axis, pairs))  426 us
    ppermute x2, waiting for transfers between devices, shards(): last = [lax.ppermute(z, 'dp', cross) for z in zgot[early:]]  146 us
    ppermute x2, waiting for transfers between devices, spread(): got = lax.ppermute(block, ('dp', 'tensor'), pairs)  83.8 us
    dot_general x4, matrix products, mm(): lax.dot_general(a, b, (((ca,), (cb,)), ((), ())), preferred_element_type=...  66.2 us
    all_gather x1, waiting for transfers between devices, shards(): col_panel = lax.all_gather(summed, 'dp', axis=0, tiled=True)  60.1 us
    dot_general x1, matrix products, shards(): jnp.einsum('jkc,rc->jrk', col_panel.reshape(n_t, kcols, mcols), summed, p...  19.4 us
  transfers between devices with their start and end apart: 17, of which 8 were waited for; matrix products, arithmetic and copies ran while one was open for 13% of the time, Pallas kernels for 0%

commit v1 on v0

--- a/solution.py
+++ b/solution.py
@@ -74,7 +74,12 @@
     early = len(zgot) // 2
     first = [lax.ppermute(z, "dp", cross) for z in zgot[:early]]
     summed, zgot, first, left_cols = lax.optimization_barrier((summed, zgot, first, left_cols))
-    col_panel = lax.all_gather(summed, "dp", axis=0, tiled=True)
+    ring = [summed]
+    for hop_ in range(7):
+        ring.append(lax.ppermute(ring[-1], "dp", [(dev, (dev + 1) % 8) for dev in range(8)]))
+    col_panel = jnp.roll(
+        jnp.concatenate(ring[::-1], axis=0), (lax.axis_index("dp") + 1) * ring[0].shape[0], axis=0
+    )
     last = [lax.ppermute(z, "dp", cross) for z in zgot[early:]]
     basis_panel = jnp.zeros((n_dp,) + right_low.shape, BF16)
     for r in range(early):

time: 909 us -> 1070 us (1.18)
  waiting for transfers between devices: 716 us -> 826 us
  local copies, waits for them, and re-layouts: 52.5 us -> 81.8 us
  starting transfers between devices: 18.9 us -> 42.9 us
    ppermute x0 -> x7, waiting for transfers between devices: none -> 315 us  [shards(): lax.ppermute(ring[-1], 'dp', [(dev, (dev + 1) % 8) for dev in range(8)])]
    ppermute x2, waiting for transfers between devices: 146 us -> 0.01 us  [shards(): last = [lax.ppermute(z, 'dp', cross) for z in zgot[early:]]]
    all_gather x1 -> x0, waiting for transfers between devices: 60.1 us -> none  [shards(): col_panel = lax.all_gather(summed, 'dp', axis=0, tiled=True)]
    unnamed x22 -> x57, local copies, waits for them, and re-layouts: 6.65 us -> 39.4 us
    ppermute x0 -> x7, starting transfers between devices: none -> 20.4 us  [shards(): lax.ppermute(ring[-1], 'dp', [(dev, (dev + 1) % 8) for dev in range(8)])]
  transfers between devices with their start and end apart: 17 -> 23, of which waited for: 8 -> 12; matrix products, arithmetic and copies ran while one was open for 13% -> 13% of each run, Pallas kernels for 0% -> 0%
where the time goes in v1:
time: 1070 us
  waiting for transfers between devices  826 us (77%)
  matrix products  82.8 us (8%)
  local copies, waits for them, and re-layouts  81.8 us (8%)
  starting transfers between devices  42.9 us (4%)
  other arithmetic  21.9 us (2%)
  between operations  14 us (1%)
    ppermute x6, waiting for transfers between devices, gather_by_permutes(): got.append(lax.ppermute(block, axis, pairs))  426 us
    ppermute x7, waiting for transfers between devices, shards(): lax.ppermute(ring[-1], 'dp', [(dev, (dev + 1) % 8) for dev in range(8)])  315 us
    ppermute x2, waiting for transfers between devices, spread(): got = lax.ppermute(block, ('dp', 'tensor'), pairs)  85.1 us
    dot_general x4, matrix products, mm(): lax.dot_general(a, b, (((ca,), (cb,)), ((), ())), preferred_element_type=...  63.8 us
    unnamed x57, local copies, waits for them, and re-layouts  39.4 us
  transfers between devices with their start and end apart: 23, of which 12 were waited for; matrix products, arithmetic and copies ran while one was open for 13% of the time, Pallas kernels for 0%

profile of v1, /device:TPU:25, one launch (start us, length us, event | category | flops | bytes accessed | tf_op | source)
XLA Modules:
  0.0 1069.8 jit_solution(18310904173520489043)
XLA Ops:
  7.2 1.8 copy-done
  9.1 19.2 %convolution_convert_fusion = bf16[4096,1536]{1,0:T(8,128)(2,1)} fusion(bf16[1024,4096]{1,0:T(8,128)(2,1)} %param.6, bf16[1024,1536]{1,0:T(8,128)(2,1)S(1)} %copy-done), kind=kOutput, calls=%fused_computation | convolution fusion | flops 12891193344 | bytes 24117248 | tf_op jit(solution)/shard_map/dot_general | solution.py:11
  28.3 2.5 broadcast_in_dim.42
  32.1 1.8 collective-permute-start.5
  34.4 22.0 %collective-permute-done.5 = bf16[512,1024]{1,0:T(8,128)(2,1)} collective-permute-done((bf16[512,1024]{1,0:T(8,128)(2,1)S(1)}, bf16[512,1024]{1,0:T(8,128)(2,1)}, u32[]{:S(2)}, u32[]{:S(2)}) %collective-permute-start.5) | collective-permute-done | bytes 1048608 | tf_op jit(solution)/shard_map/ppermute | solution.py:39
  56.3 2.3 bitcast_dynamic-update-slice_fusion.10
  58.6 21.3 %collective-permute-done.6 = bf16[512,1024]{1,0:T(8,128)(2,1)S(1)} collective-permute-done((bf16[512,1024]{1,0:T(8,128)(2,1)S(1)}, bf16[512,1024]{1,0:T(8,128)(2,1)S(1)}, u32[]{:S(2)}, u32[]{:S(2)}) %collective-permute-start.6) | collective-permute-done | bytes 1048608 | tf_op jit(solution)/shard_map/ppermute | solution.py:39
  82.0 2.5 fusion.6
  84.5 2.3 pad_maximum_fusion
  86.8 5.6 all-to-all-start
  92.4 2.6 convert_element_type.22
  98.0 159.0 %collective-permute-done = bf16[768,1536]{1,0:T(8,128)(2,1)S(1)} collective-permute-done((bf16[768,1536]{1,0:T(8,128)(2,1)S(1)}, bf16[768,1536]{1,0:T(8,128)(2,1)S(1)}, u32[]{:S(2)}, u32[]{:S(2)}) %collective-permute-start) | collective-permute-done | bytes 2359328 | tf_op jit(solution)/shard_map/ppermute | solution.py:39
  258.1 224.0 %collective-permute-done.1 = bf16[768,1536]{1,0:T(8,128)(2,1)S(1)} collective-permute-done((bf16[768,1536]{1,0:T(8,128)(2,1)S(1)}, bf16[768,1536]{1,0:T(8,128)(2,1)S(1)}, u32[]{:S(2)}, u32[]{:S(2)}) %collective-permute-start.1) | collective-permute-done | bytes 2359328 | tf_op jit(solution)/shard_map/ppermute | solution.py:39
  485.7 1.5 collective-permute-start.8
  487.2 35.3 %collective-permute-done.8 = bf16[512,1536]{1,0:T(8,128)(2,1)S(1)} collective-permute-done((bf16[512,1536]{1,0:T(8,128)(2,1)}, bf16[512,1536]{1,0:T(8,128)(2,1)S(1)}, u32[]{:S(2)}, u32[]{:S(2)}) %collective-permute-start.8) | collective-permute-done | bytes 1572896 | tf_op jit(solution)/shard_map/ppermute | solution.py:79
  524.1 35.0 %collective-permute-done.9 = bf16[512,1536]{1,0:T(8,128)(2,1)S(1)} collective-permute-done((bf16[512,1536]{1,0:T(8,128)(2,1)S(1)}, bf16[512,1536]{1,0:T(8,128)(2,1)S(1)}, u32[]{:S(2)}, u32[]{:S(2)}) %collective-permute-start.9) | collective-permute-done | bytes 1572896 | tf_op jit(solution)/shard_map/ppermute | solution.py:79
  561.1 33.9 %collective-permute-done.10 = bf16[512,1536]{1,0:T(8,128)(2,1)S(1)} collective-permute-done((bf16[512,1536]{1,0:T(8,128)(2,1)S(1)}, bf16[512,1536]{1,0:T(8,128)(2,1)S(1)}, u32[]{:S(2)}, u32[]{:S(2)}) %collective-permute-start.10) | collective-permute-done | bytes 1572896 | tf_op jit(solution)/shard_map/ppermute | solution.py:79
  596.1 2.9 collective-permute-start.11
  599.0 30.9 %collective-permute-done.11 = bf16[512,1536]{1,0:T(8,128)(2,1)S(1)} collective-permute-done((bf16[512,1536]{1,0:T(8,128)(2,1)S(1)}, bf16[512,1536]{1,0:T(8,128)(2,1)S(1)}, u32[]{:S(2)}, u32[]{:S(2)}) %collective-permute-start.11) | collective-permute-done | bytes 1572896 | tf_op jit(solution)/shard_map/ppermute | solution.py:79
  631.1 4.9 collective-permute-start.12
  636.0 30.0 %collective-permute-done.12 = bf16[512,1536]{1,0:T(8,128)(2,1)} collective-permute-done((bf16[512,1536]{1,0:T(8,128)(2,1)S(1)}, bf16[512,1536]{1,0:T(8,128)(2,1)}, u32[]{:S(2)}, u32[]{:S(2)}) %collective-permute-start.12) | collective-permute-done | bytes 1572896 | tf_op jit(solution)/shard_map/ppermute | solution.py:79
  666.0 4.9 collective-permute-start.13
  670.9 5.0 collective-permute-start.15
  676.0 1.7 broadcast_in_dim.47
  677.9 22.4 %collective-permute-done.13 = bf16[512,1536]{1,0:T(8,128)(2,1)} collective-permute-done((bf16[512,1536]{1,0:T(8,128)(2,1)}, bf16[512,1536]{1,0:T(8,128)(2,1)}, u32[]{:S(2)}, u32[]{:S(2)}) %collective-permute-start.13) | collective-permute-done | bytes 1572896 | tf_op jit(solution)/shard_map/ppermute | solution.py:79
  700.4 4.9 collective-permute-start.14
  705.8 2.0 bitcast_dynamic-update-slice_fusion.4
  707.9 127.3 %collective-permute-done.14 = bf16[512,1536]{1,0:T(8,128)(2,1)S(1)} collective-permute-done((bf16[512,1536]{1,0:T(8,128)(2,1)}, bf16[512,1536]{1,0:T(8,128)(2,1)S(1)}, u32[]{:S(2)}, u32[]{:S(2)}) %collective-permute-start.14) | collective-permute-done | bytes 1572896 | tf_op jit(solution)/shard_map/ppermute | solution.py:79
  836.4 2.8 constant_dynamic-update-slice_fusion.14
  839.2 2.8 constant_dynamic-update-slice_fusion.13
  849.7 2.7 constant_dynamic-update-slice_fusion.6
  852.4 2.7 constant_dynamic-update-slice_fusion.5
  861.3 6.1 constant_dynamic-slice_fusion.1
  867.5 4.5 copy-done.2
  872.0 9.3 convolution_convert_fusion.1
  881.4 9.6 constant_dynamic-slice_fusion
  891.0 1.5 collective-permute-start.17
  892.5 19.0 %convert_bitcast_fusion = bf16[4,512,1024]{2,1,0:T(8,128)(2,1)} fusion(bf16[4,1024,1536]{2,1,0:T(8,128)(2,1)} %bitcast.42, bf16[512,1536]{1,0:T(8,128)(2,1)S(1)} %copy-done.4), kind=kOutput, calls=%fused_computation.7 | convolution fusion | flops 6444548096 | bytes 18350080 | tf_op jit(solution)/shard_map/jkc,rc->jrk/dot_general | solution.py:99
  911.6 85.1 %collective-permute-done.17 = bf16[4096,768]{1,0:T(8,128)(2,1)} collective-permute-done((bf16[4096,768]{1,0:T(8,128)(2,1)}, bf16[4096,768]{1,0:T(8,128)(2,1)}, u32[]{:S(2)}, u32[]{:S(2)}) %collective-permute-start.17) | collective-permute-done | bytes 6291488 | tf_op jit(solution)/shard_map/ppermute | solution.py:24
  996.7 12.0 %broadcast_select_fusion = bf16[4096,768]{1,0:T(8,128)(2,1)} fusion(bf16[4096,768]{1,0:T(8,128)(2,1)} %collective-permute-done.17, pred[]{:T(512)S(6)} %eq.13, bf16[4096,1536]{1,0:T(8,128)(2,1)} %copy-done.2, s32[]{:T(128)S(6)} %select_n.95), kind=kLoop, calls=%fused_computation.3 | loop fusion | flops 3145728 | bytes 18874372 | tf_op jit(solution)/shard_map/jit(_where)/select_n | solution.py:27
  1008.7 4.0 collective-permute-start.18
  1012.7 3.4 bitcast_dynamic-update-slice_fusion.3
  1016.2 3.2 bitcast_dynamic-update-slice_fusion.2
  1019.4 1.6 bitcast_dynamic-update-slice_fusion.1
  1021.0 3.3 bitcast_dynamic-update-slice_fusion
  1024.3 17.0 %fusion.7 = f32[512,1536]{1,0:T(8,128)} fusion(bf16[512,6144]{1,0:T(8,128)(2,1)} %all-gather.2.cloned.1.call-done, bf16[6144,1536]{1,0:T(8,128)(2,1)} %bitcast.43), kind=kOutput, calls=%fused_computation.42 | convolution fusion | flops 9663676416 | bytes 28311552 | tf_op jit(solution)/shard_map/dot_general | solution.py:11
  1041.2 18.3 %multiply_add_fusion = f32[768,1536]{1,0:T(8,128)} fusion(f32[768,1536]{1,0:T(8,128)} %param.9, bf16[4096,1536]{1,0:T(8,128)(2,1)} %copy-done.2, bf16[4096,768]{1,0:T(8,128)(2,1)} %collective-permute-done.18, bf16[4096,768]{1,0:T(8,128)(2,1)} %broadcast_select_fusion, pred[]{:T(512)S(6)} %eq.12), kind=kOutput, calls=%fused_computation.5 | convolution fusion | flops 9670361088 | bytes 34603008 | tf_op jit(solution)/shard_map/dot_general | solution.py:11
  1059.5 3.7 multiply_add_fusion.1
  (85 shorter events, 33.5 us)
Async XLA Ops:
  7.2 1.9 copy-start
  7.2 478.5 %reduce-scatter.3.cloned.1.call-start = ((), (), s32[]{:S(2)}) async-start(), calls=%async_computation.3 | async-start | bytes 14155776 | tf_op jit(solution)/shard_map/reduce_scatter | solution.py:62
  28.3 2.6 copy-start.20
  32.1 24.2 %collective-permute-start.5 = (bf16[512,1024]{1,0:T(8,128)(2,1)S(1)}, bf16[512,1024]{1,0:T(8,128)(2,1)}, u32[]{:S(2)}, u32[]{:S(2)}) collective-permute-start(bf16[512,1024]{1,0:T(8,128)(2,1)S(1)} %get-tuple-element.36), channel_id=1, source_target_pairs={{0,1},{1,2},{2,3},{3,0},{4,5},{5,6},{6,7},{7,4},{8,9},{9,10},{10,1... | collective-permute-start | bytes 3145736 | tf_op jit(solution)/shard_map/ppermute | solution.py:39
  33.9 46.0 %collective-permute-start.6 = (bf16[512,1024]{1,0:T(8,128)(2,1)S(1)}, bf16[512,1024]{1,0:T(8,128)(2,1)S(1)}, u32[]{:S(2)}, u32[]{:S(2)}) collective-permute-start(bf16[512,1024]{1,0:T(8,128)(2,1)S(1)} %get-tuple-element.36), channel_id=1, source_target_pairs={{0,2},{1,3},{2,0},{3,1},{4,6},{5,7},{6,4},{7,5},{8,10},{9,11},{10,... | collective-permute-start | bytes 3145736 | tf_op jit(solution)/shard_map/ppermute | solution.py:39
  34.1 46.8 %collective-permute-start.7 = (bf16[512,1024]{1,0:T(8,128)(2,1)S(1)}, bf16[512,1024]{1,0:T(8,128)(2,1)S(1)}, u32[]{:S(2)}, u32[]{:S(2)}) collective-permute-start(bf16[512,1024]{1,0:T(8,128)(2,1)S(1)} %get-tuple-element.36), channel_id=1, source_target_pairs={{0,3},{1,0},{2,1},{3,2},{4,7},{5,4},{6,5},{7,6},{8,11},{9,8},{10,9... | collective-permute-start | bytes 3145736 | tf_op jit(solution)/shard_map/ppermute | solution.py:39
  86.8 398.9 %all-to-all-start = ((bf16[8,512,512]{2,1,0:T(8,128)(2,1)}), bf16[8,512,512]{2,1,0:T(8,128)(2,1)}, u32[]{:S(2)}, u32[]{:S(2)}) async-start(bf16[8,512,512]{2,1,0:T(8,128)(2,1)} %bitcast.44), calls=%async_computation.1 | async-start | bytes 8388608 | tf_op jit(solution)/shard_map/all_to_all | solution.py:64
  92.4 931.9 %all-gather.2.cloned.1.call-start = ((), (), s32[]{:S(2)}) async-start(), calls=%async_computation.5 | async-start | bytes 7864320 | tf_op jit(solution)/shard_map/all_gather | solution.py:97
  95.0 162.0 %collective-permute-start = (bf16[768,1536]{1,0:T(8,128)(2,1)S(1)}, bf16[768,1536]{1,0:T(8,128)(2,1)S(1)}, u32[]{:S(2)}, u32[]{:S(2)}) collective-permute-start(bf16[768,1536]{1,0:T(8,128)(2,1)S(1)} %convert_element_type.22), channel_id=1, source_target_pairs={{0,8},{4,12},{8,16},{12,20},{16,24},{20,28},{24,0},{28,4},{1,9},{5... | collective-permute-start | bytes 7077896 | tf_op jit(solution)/shard_map/ppermute | solution.py:39
  95.2 386.9 %collective-permute-start.1 = (bf16[768,1536]{1,0:T(8,128)(2,1)S(1)}, bf16[768,1536]{1,0:T(8,128)(2,1)S(1)}, u32[]{:S(2)}, u32[]{:S(2)}) collective-permute-start(bf16[768,1536]{1,0:T(8,128)(2,1)S(1)} %convert_element_type.22), channel_id=1, source_target_pairs={{0,16},{4,20},{8,24},{12,28},{16,0},{20,4},{24,8},{28,12},{1,17},{... | collective-permute-start | bytes 7077896 | tf_op jit(solution)/shard_map/ppermute | solution.py:39
  96.5 385.6 %collective-permute-start.2 = (bf16[768,1536]{1,0:T(8,128)(2,1)S(1)}, bf16[768,1536]{1,0:T(8,128)(2,1)S(1)}, u32[]{:S(2)}, u32[]{:S(2)}) collective-permute-start(bf16[768,1536]{1,0:T(8,128)(2,1)S(1)} %convert_element_type.22), channel_id=1, source_target_pairs={{0,24},{4,28},{8,0},{12,4},{16,8},{20,12},{24,16},{28,20},{1,25},{... | collective-permute-start | bytes 7077896 | tf_op jit(solution)/shard_map/ppermute | solution.py:39
  96.8 385.3 %collective-permute-start.3 = (bf16[768,1536]{1,0:T(8,128)(2,1)S(1)}, bf16[768,1536]{1,0:T(8,128)(2,1)S(1)}, u32[]{:S(2)}, u32[]{:S(2)}) collective-permute-start(bf16[768,1536]{1,0:T(8,128)(2,1)S(1)} %convert_element_type.22), channel_id=1, source_target_pairs={{0,4},{4,0},{8,12},{12,8},{16,20},{20,16},{24,28},{28,24},{1,5},{5... | collective-permute-start | bytes 7077896 | tf_op jit(solution)/shard_map/ppermute | solution.py:75
  256.9 225.2 %copy-start.16 = (bf16[768,1536]{1,0:T(8,128)(2,1)}, bf16[768,1536]{1,0:T(8,128)(2,1)S(1)}, u32[]{:S(2)}) copy-start(bf16[768,1536]{1,0:T(8,128)(2,1)S(1)} %collective-permute-done) | copy-start | bytes 7077892
  256.9 228.8 %collective-permute-start.4 = (bf16[768,1536]{1,0:T(8,128)(2,1)S(1)}, bf16[768,1536]{1,0:T(8,128)(2,1)}, u32[]{:S(2)}, u32[]{:S(2)}) collective-permute-start(bf16[768,1536]{1,0:T(8,128)(2,1)S(1)} %collective-permute-done), channel_id=1, source_target_pairs={{0,4},{4,0},{8,12},{12,8},{16,20},{20,16},{24,28},{28,24},{1,5},{5... | collective-permute-start | bytes 7077896 | tf_op jit(solution)/shard_map/ppermute | solution.py:75
  482.1 1.5 copy-start.15
  482.1 2.2 copy-start.13
  484.3 1.4 copy-start.18
  485.7 36.7 %collective-permute-start.8 = (bf16[512,1536]{1,0:T(8,128)(2,1)}, bf16[512,1536]{1,0:T(8,128)(2,1)S(1)}, u32[]{:S(2)}, u32[]{:S(2)}) collective-permute-start(bf16[512,1536]{1,0:T(8,128)(2,1)} %reduce-scatter.3.cloned.1.call-done), channel_id=1, source_target_pairs={{0,4},{4,8},{8,12},{12,16},{16,20},{20,24},{24,28},{28,0},{1,5},{5... | collective-permute-start | bytes 4718600 | tf_op jit(solution)/shard_map/ppermute | solution.py:79
  522.5 1.2 copy-start.5
  523.6 35.6 %collective-permute-start.9 = (bf16[512,1536]{1,0:T(8,128)(2,1)S(1)}, bf16[512,1536]{1,0:T(8,128)(2,1)S(1)}, u32[]{:S(2)}, u32[]{:S(2)}) collective-permute-start(bf16[512,1536]{1,0:T(8,128)(2,1)S(1)} %collective-permute-done.8), channel_id=1, source_target_pairs={{0,4},{4,8},{8,12},{12,16},{16,20},{20,24},{24,28},{28,0},{1,5},{5... | collective-permute-start | bytes 4718600 | tf_op jit(solution)/shard_map/ppermute | solution.py:79
  559.2 1.1 copy-start.7
  560.3 34.6 %collective-permute-start.10 = (bf16[512,1536]{1,0:T(8,128)(2,1)S(1)}, bf16[512,1536]{1,0:T(8,128)(2,1)S(1)}, u32[]{:S(2)}, u32[]{:S(2)}) collective-permute-start(bf16[512,1536]{1,0:T(8,128)(2,1)S(1)} %collective-permute-done.9), channel_id=1, source_target_pairs={{0,4},{4,8},{8,12},{12,16},{16,20},{20,24},{24,28},{28,0},{1,5},{5... | collective-permute-start | bytes 4718600 | tf_op jit(solution)/shard_map/ppermute | solution.py:79
  595.0 1.1 copy-start.9
  596.1 33.9 %collective-permute-start.11 = (bf16[512,1536]{1,0:T(8,128)(2,1)S(1)}, bf16[512,1536]{1,0:T(8,128)(2,1)S(1)}, u32[]{:S(2)}, u32[]{:S(2)}) collective-permute-start(bf16[512,1536]{1,0:T(8,128)(2,1)S(1)} %collective-permute-done.10), channel_id=1, source_target_pairs={{0,4},{4,8},{8,12},{12,16},{16,20},{20,24},{24,28},{28,0},{1,5},{5... | collective-permute-start | bytes 4718600 | tf_op jit(solution)/shard_map/ppermute | solution.py:79
  630.0 1.1 copy-start.11
  631.1 34.9 %collective-permute-start.12 = (bf16[512,1536]{1,0:T(8,128)(2,1)S(1)}, bf16[512,1536]{1,0:T(8,128)(2,1)}, u32[]{:S(2)}, u32[]{:S(2)}) collective-permute-start(bf16[512,1536]{1,0:T(8,128)(2,1)S(1)} %collective-permute-done.11), channel_id=1, source_target_pairs={{0,4},{4,8},{8,12},{12,16},{16,20},{20,24},{24,28},{28,0},{1,5},{5... | collective-permute-start | bytes 4718600 | tf_op jit(solution)/shard_map/ppermute | solution.py:79
  666.0 34.3 %collective-permute-start.13 = (bf16[512,1536]{1,0:T(8,128)(2,1)}, bf16[512,1536]{1,0:T(8,128)(2,1)}, u32[]{:S(2)}, u32[]{:S(2)}) collective-permute-start(bf16[512,1536]{1,0:T(8,128)(2,1)} %collective-permute-done.12), channel_id=1, source_target_pairs={{0,4},{4,8},{8,12},{12,16},{16,20},{20,24},{24,28},{28,0},{1,5},{5... | collective-permute-start | bytes 4718600 | tf_op jit(solution)/shard_map/ppermute | solution.py:79
  670.9 196.6 %collective-permute-start.15 = (bf16[768,1536]{1,0:T(8,128)(2,1)}, bf16[768,1536]{1,0:T(8,128)(2,1)}, u32[]{:S(2)}, u32[]{:S(2)}) collective-permute-start(bf16[768,1536]{1,0:T(8,128)(2,1)} %copy-done.15), channel_id=1, source_target_pairs={{0,4},{4,0},{8,12},{12,8},{16,20},{20,16},{24,28},{28,24},{1,5},{5... | collective-permute-start | bytes 7077896 | tf_op jit(solution)/shard_map/ppermute | solution.py:83
  675.9 191.6 %collective-permute-start.16 = (bf16[768,1536]{1,0:T(8,128)(2,1)}, bf16[768,1536]{1,0:T(8,128)(2,1)}, u32[]{:S(2)}, u32[]{:S(2)}) collective-permute-start(bf16[768,1536]{1,0:T(8,128)(2,1)} %copy-done.13), channel_id=1, source_target_pairs={{0,4},{4,0},{8,12},{12,8},{16,20},{20,16},{24,28},{28,24},{1,5},{5... | collective-permute-start | bytes 7077896 | tf_op jit(solution)/shard_map/ppermute | solution.py:83
  677.6 27.6 %copy-start.19 = (bf16[768,1536]{1,0:T(8,128)(2,1)S(1)}, bf16[768,1536]{1,0:T(8,128)(2,1)}, u32[]{:S(2)}) copy-start(bf16[768,1536]{1,0:T(8,128)(2,1)} %copy-done.18) | copy-start | bytes 7077892
  677.7 27.9 %copy-start.17 = (bf16[768,1536]{1,0:T(8,128)(2,1)S(1)}, bf16[768,1536]{1,0:T(8,128)(2,1)}, u32[]{:S(2)}) copy-start(bf16[768,1536]{1,0:T(8,128)(2,1)} %copy-done.16) | copy-start | bytes 7077892
  700.4 134.8 %collective-permute-start.14 = (bf16[512,1536]{1,0:T(8,128)(2,1)}, bf16[512,1536]{1,0:T(8,128)(2,1)S(1)}, u32[]{:S(2)}, u32[]{:S(2)}) collective-permute-start(bf16[512,1536]{1,0:T(8,128)(2,1)} %collective-permute-done.13), channel_id=1, source_target_pairs={{0,4},{4,8},{8,12},{12,16},{16,20},{20,24},{24,28},{28,0},{1,5},{5... | collective-permute-start | bytes 4718600 | tf_op jit(solution)/shard_map/ppermute | solution.py:79
  705.8 136.3 %copy-start.12 = (bf16[512,1536]{1,0:T(8,128)(2,1)S(1)}, bf16[512,1536]{1,0:T(8,128)(2,1)}, u32[]{:S(2)}) copy-start(bf16[512,1536]{1,0:T(8,128)(2,1)} %copy-done.11) | copy-start | bytes 4718596
  707.9 149.7 %copy-start.3 = (bf16[8,768,1536]{2,1,0:T(8,128)(2,1)}, bf16[8,768,1536]{2,1,0:T(8,128)(2,1)S(1)}, u32[]{:S(2)}) copy-start(bf16[8,768,1536]{2,1,0:T(8,128)(2,1)S(1)} %bitcast_dynamic-update-slice_fusion.4) | copy-start | bytes 56623108
  707.9 135.4 %copy-start.10 = (bf16[512,1536]{1,0:T(8,128)(2,1)S(1)}, bf16[512,1536]{1,0:T(8,128)(2,1)}, u32[]{:S(2)}) copy-start(bf16[512,1536]{1,0:T(8,128)(2,1)} %copy-done.9) | copy-start | bytes 4718596
  836.4 8.1 copy-start.8
  839.2 6.6 copy-start.6
  842.1 5.2 copy-start.4
  867.5 4.5 copy-start.2
  881.3 178.2 %reduce-scatter.5.cloned.1.call-start = ((), (), s32[]{:S(2)}) async-start(), calls=%async_computation.4 | async-start | bytes 5242880 | tf_op jit(solution)/shard_map/reduce_scatter | solution.py:103
  891.0 105.7 %collective-permute-start.17 = (bf16[4096,768]{1,0:T(8,128)(2,1)}, bf16[4096,768]{1,0:T(8,128)(2,1)}, u32[]{:S(2)}, u32[]{:S(2)}) collective-permute-start(bf16[4096,768]{1,0:T(8,128)(2,1)} %constant_dynamic-slice_fusion), channel_id=1, source_target_pairs={{0,2},{4,6},{9,11},{13,15},{18,16},{22,20},{27,25},{31,29}} | collective-permute-start | bytes 18874376 | tf_op jit(solution)/shard_map/ppermute | solution.py:24
  1008.7 32.5 %collective-permute-start.18 = (bf16[4096,768]{1,0:T(8,128)(2,1)}, bf16[4096,768]{1,0:T(8,128)(2,1)}, u32[]{:S(2)}, u32[]{:S(2)}) collective-permute-start(bf16[4096,768]{1,0:T(8,128)(2,1)} %broadcast_select_fusion), channel_id=1, source_target_pairs={{0,1},{2,3},{4,5},{6,7},{9,8},{11,10},{13,12},{15,14},{18,19},{16,... | collective-permute-start | bytes 18874376 | tf_op jit(solution)/shard_map/ppermute | solution.py:24
  1012.7 6.7 copy-start.14
  1041.2 22.0 %copy-start.1 = (bf16[1024,1536]{1,0:T(8,128)(2,1)S(1)}, bf16[1024,1536]{1,0:T(8,128)(2,1)}, u32[]{:S(2)}) copy-start(bf16[1024,1536]{1,0:T(8,128)(2,1)} %param.7) | copy-start | bytes 9437188
Sparse Core Ops, SparseCore 0:
  28.4 407.5 reduce-scatter.2
  881.4 70.9 all-gather.1
  1012.8 45.7 reduce-scatter.4
